TPU v7x, 32 devices: a whole 2x2x4 slice. The times are simulated.
32 devices in a mesh: src: 4 (over y, core), dst: 8 (over z, x).
Axes of the slice: x: 2, y: 2, z: 4, core: 2. Of those that a mesh axis runs over, the one named last changes fastest.
Arguments:
- features: bfloat16 [8192, 768], P(('src', 'dst')), may hold values from -6 to 6
- edge_tiles: bfloat16 [4, 8, 64, 128, 128], P('src', 'dst'), may hold values from -0.3125 to 0.3125
- tile_src: int32 [4, 8, 64], P('src', 'dst'), may hold values from 0 to 7
- tile_dst: int32 [4, 8, 64], P('src', 'dst'), may hold values from 0 to 15, as said below
- tile_count: int32 [4, 8], P('src', 'dst'), may hold values from 1 to 64, as said below
- weight: bfloat16 [768, 1024], replicated, may hold values from -0.21875 to 0.21875
- out_bias: float32 [1024], replicated, may hold values from -3 to 3
- out_grad: bfloat16 [8192, 1024], P(('src', 'dst')), may hold values from -6 to 6
Outputs:
- hidden: bfloat16 [8192, 1024], P(('src', 'dst'))
- feature_grad: bfloat16 [8192, 768], P(('src', 'dst'))
- weight_grad: float32 [768, 1024], replicated
- bias_grad: float32 [1024], replicated
Inputs may be any that keep to these rules, and one draw needn't show every extreme that they name: `tile_src`: block s of the source column of device (i, k) is block s % 2 of device (s // 2, k). `tile_dst`: block e of the destination row of device (i, k) is block e % 2 of device (i, e // 2). On one device, all tile slots whose destination blocks lie on one device name the same block. In every row of devices, slot 0 of every device names one common block. `tile_count`: some device uses all 64 slots.
All inputs are finite; a program needn't handle non-finite values.
Results may differ from a plain program's by a relative error of at most 0.024.
Values may be sent and summed in bfloat16 or wider, within the bound.
A program may use at most 128 MiB of HBM per device.

v0:
```python
import jax
import jax.numpy as jnp
from jax import lax
from jax.sharding import PartitionSpec as P


def per_device(features, edge_tiles, tile_src, tile_dst, tile_count, weight, out_bias, out_grad):
    capacity = edge_tiles.shape[2]
    edge_size = edge_tiles.shape[3]
    feat_width = features.shape[1]
    block_rows = features.shape[0]
    blocks = block_rows // edge_size
    masters = lax.axis_size("dst")
    holders = lax.axis_size("src")
    adjacency = edge_tiles.reshape(capacity, edge_size, edge_size)
    src_ids = tile_src.reshape(capacity)
    dst_ids = tile_dst.reshape(capacity)
    tile_total = tile_count.reshape(())
    alive_mask = jnp.arange(capacity, dtype=jnp.int32) < tile_total
    block_ids = jnp.arange(blocks, dtype=jnp.int32)
    owner_ids = dst_ids // blocks
    inner_ids = dst_ids % blocks
    column = lax.all_gather(features, "src", axis=0, tiled=True).reshape(
        holders * blocks, edge_size, feat_width
    )
    picked = column[src_ids]
    partial_value = jnp.einsum(
        "tij,tjf->tif", adjacency, picked, preferred_element_type=jnp.float32
    )
    routing = (owner_ids[None, :] == jnp.arange(masters, dtype=jnp.int32)[:, None]) & alive_mask[
        None, :
    ]
    outgoing = jnp.einsum("pt,tif->pif", routing.astype(jnp.float32), partial_value)
    wanted_block = jnp.max(jnp.where(routing, inner_ids[None, :], 0), axis=1)
    wanted_rows = jnp.broadcast_to(wanted_block[:, None], (masters, edge_size))
    incoming = lax.all_to_all(
        outgoing.astype(jnp.bfloat16), "dst", split_axis=0, concat_axis=0, tiled=True
    )
    asked = lax.all_to_all(wanted_rows, "dst", split_axis=0, concat_axis=0, tiled=True)
    chooser = (asked[None, :, :] == block_ids[:, None, None]).astype(jnp.bfloat16)
    aggregate = jnp.einsum(
        "jpr,prf->jrf", chooser, incoming, preferred_element_type=jnp.float32
    ).astype(jnp.bfloat16)
    preact = (
        jnp.einsum("jrf,fh->jrh", aggregate, weight, preferred_element_type=jnp.float32) + out_bias
    )
    aggregate, preact, asked = (aggregate, preact, asked)
    gate_value = jax.nn.sigmoid(preact)
    hidden = (preact * gate_value).astype(jnp.bfloat16).reshape(block_rows, -1)
    grad_in = out_grad.reshape(blocks, edge_size, -1).astype(jnp.float32)
    pre_grad = grad_in * (gate_value * (1.0 + preact * (1.0 - gate_value)))
    pre_grad_b = pre_grad.astype(jnp.bfloat16)
    weight_term = jnp.einsum(
        "jrf,jrh->fh", aggregate, pre_grad_b, preferred_element_type=jnp.float32
    )
    bias_term = jnp.sum(pre_grad, axis=(0, 1))
    weight_grad, bias_grad = lax.psum((weight_term, bias_term), ("src", "dst"))
    back = jnp.einsum("jrh,fh->jrf", pre_grad_b, weight, preferred_element_type=jnp.float32).astype(
        jnp.bfloat16
    )
    asked_block = asked[:, 0]
    selector = (asked_block[:, None] == block_ids[None, :]).astype(jnp.bfloat16)
    replies = jnp.einsum("pj,jrf->prf", selector, back, preferred_element_type=jnp.float32).astype(
        jnp.bfloat16
    )
    returned = lax.all_to_all(replies, "dst", split_axis=0, concat_axis=0, tiled=True)
    wanted = returned[owner_ids]
    source = jnp.einsum("tji,tjf->tif", adjacency, wanted, preferred_element_type=jnp.float32)
    src_routing = (
        src_ids[None, :] == jnp.arange(holders * blocks, dtype=jnp.int32)[:, None]
    ) & alive_mask[None, :]
    src_terms = jnp.einsum("kt,tif->kif", src_routing.astype(jnp.float32), source)
    summed = lax.psum_scatter(
        src_terms.reshape(holders * block_rows, feat_width).astype(jnp.bfloat16),
        "src",
        scatter_dimension=0,
        tiled=True,
    )
    return (hidden, summed, weight_grad, bias_grad)


def solution(mesh):
    in_specs = (
        P(("src", "dst"), None),
        P("src", "dst", None, None, None),
        P("src", "dst", None),
        P("src", "dst", None),
        P("src", "dst"),
        P(),
        P(),
        P(("src", "dst"), None),
    )
    out_specs = (P(("src", "dst"), None), P(("src", "dst"), None), P(), P())
    return jax.shard_map(
        per_device, mesh=mesh, in_specs=in_specs, out_specs=out_specs, check_vma=False
    )
```

profile of v0, /device:TPU:0, one launch (start us, length us, event | category | flops | bytes accessed | tf_op | source)
XLA Modules:
  0.0 330.1 jit_solution(10724298226550727925)
XLA Ops:
  7.2 0.7 all-gather.2.cloned.1.call-update
  8.6 0.7 and_select_fusion.1
  9.4 0.7 broadcast_in_dim.16
  10.0 7.3 %all-to-all-start.1 = ((s32[8,1,128]{2,1,0:T(1,128)}), s32[8,1,128]{2,1,0:T(1,128)S(1)}, u32[]{:S(2)}, u32[]{:S(2)}) async-start(s32[8,1,128]{2,1,0:T(1,128)} %broadcast_in_dim.16), calls=%async_computation.1 | async-start | bytes 8192 | tf_op jit(solution)/shard_map/all_to_all | solution.py:39
  17.3 0.7 fusion.39
  18.0 14.0 %all-gather.2.cloned.1.call-done = bf16[1024,768]{1,0:T(8,128)(2,1)} async-done(((bf16[256,768]{1,0:T(8,128)(2,1)}), bf16[1024,768]{1,0:T(8,128)(2,1)}) %all-gather.2.cloned.1.call-update) | async-done | bytes 1572880 | tf_op jit(solution)/shard_map/all_gather | solution.py:23
  31.9 8.6 %gather_fusion = bf16[64,128,768]{2,1,0:T(8,128)(2,1)} fusion(bf16[8,128,768]{2,1,0:T(8,128)(2,1)} %bitcast.81, s32[1024]{0:T(1024)S(1)} %pad_clamp_fusion.1), kind=kCustom, calls=%fused_computation | custom fusion | bytes 25166080 | tf_op jit(solution)/shard_map/gather | solution.py:26
  40.6 9.1 %convolution_bitcast_fusion.1 = bf16[64,128,768]{1,2,0:T(8,128)(2,1)} fusion(bf16[64,128,768]{2,1,0:T(8,128)(2,1)} %gather_fusion, bf16[1,1,64,128,128]{4,3,2,1,0:T(8,128)(2,1)S(1)} %copy-done), kind=kOutput, calls=%fused_computation.3 | convolution fusion | flops 1610612736 | bytes 27262976 | tf_op jit(solution)/shard_map/tij,tjf->tif/dot_general | solution.py:27
  49.7 16.8 %copy.40 = bf16[64,128,768]{2,0,1:T(8,128)(2,1)} copy(bf16[64,128,768]{1,2,0:T(8,128)(2,1)} %convolution_bitcast_fusion.1) | data formatting | bytes 25165824 | tf_op jit(solution)/shard_map/tij,tjf->tif/dot_general | solution.py:27
  66.5 6.3 %convolution_convert_fusion.2 = bf16[8,128,768]{2,0,1:T(8,128)(2,1)S(1)} fusion(bf16[64,128,768]{2,0,1:T(8,128)(2,1)} %copy.40, s32[64]{0:T(128)S(1)} %get-tuple-element.8, pred[64]{0:T(512)(128)(4,1)S(1)} %iota_compare_fusion.2), kind=kOutput, calls=%fused_computation.9 | convolution fusion | flops 100664320 | bytes 14156096 | tf_op jit(solution)/shard_map/pt,tif->pif/dot_general | solution.py:33
  72.8 1.5 copy.41
  74.3 5.6 %all-to-all-start = ((bf16[8,128,768]{2,1,0:T(8,128)(2,1)}), bf16[8,128,768]{2,1,0:T(8,128)(2,1)}, u32[]{:S(2)}, u32[]{:S(2)}) async-start(bf16[8,128,768]{2,1,0:T(8,128)(2,1)} %copy.41), calls=%async_computation | async-start | bytes 3145728 | tf_op jit(solution)/shard_map/all_to_all | solution.py:36
  80.1 37.2 %all-to-all-done = bf16[8,128,768]{2,1,0:T(8,128)(2,1)} async-done(((bf16[8,128,768]{2,1,0:T(8,128)(2,1)}), bf16[8,128,768]{2,1,0:T(8,128)(2,1)}, u32[]{:S(2)}, u32[]{:S(2)}) %all-to-all-start) | async-done | bytes 1572896 | tf_op jit(solution)/shard_map/all_to_all | solution.py:36
  117.3 2.6 fusion.17
  119.8 0.5 copy.50
  120.3 3.3 %fusion.42 = (f32[1024]{0:T(1024)S(1)}, bf16[2,128,1024]{2,1,0:T(8,128)(2,1)S(1)}, bf16[2,128,1024]{2,1,0:T(8,128)(2,1)}) fusion(bf16[2,128,1024]{2,1,0:T(8,128)(2,1)S(1)} %bitcast.86, f32[1024]{0:T(1024)S(1)} %copy-done.4, bf16[2,128,768]{1,2,0:T(8,128)(2,1)S(1)} %copy.50, bf16[768,1024]{1,0:T(8,128)(2,1)} %param.13), kind=kOutput, calls=%fused_computation.63 | convolution fusion | flops 406322176 | bytes 3547136 | tf_op jit(solution)/shard_map/jrf,fh->jrh/dot_general | solution.py:45
  123.7 0.7 fusion.14
  124.3 0.7 convolution_convert_fusion.1
  125.0 1.4 copy.46
  126.5 4.4 %all-to-all-start.2 = ((bf16[8,128,768]{2,1,0:T(8,128)(2,1)}), bf16[8,128,768]{2,1,0:T(8,128)(2,1)}, u32[]{:S(2)}, u32[]{:S(2)}) async-start(bf16[8,128,768]{2,1,0:T(8,128)(2,1)} %copy.46), calls=%async_computation.2 | async-start | bytes 3145728 | tf_op jit(solution)/shard_map/all_to_all | solution.py:66
  131.0 2.2 convolution_bitcast_fusion.2
  133.3 0.2 reduce-scatter.2.cloned.1.call-start
  133.5 44.2 %all-to-all-done.2 = bf16[8,128,768]{2,1,0:T(8,128)(2,1)} async-done(((bf16[8,128,768]{2,1,0:T(8,128)(2,1)}), bf16[8,128,768]{2,1,0:T(8,128)(2,1)}, u32[]{:S(2)}, u32[]{:S(2)}) %all-to-all-start.2) | async-done | bytes 1572896 | tf_op jit(solution)/shard_map/all_to_all | solution.py:66
  177.7 8.6 %gather_fusion.1 = bf16[64,128,768]{2,1,0:T(8,128)(2,1)} fusion(bf16[8,128,768]{2,1,0:T(8,128)(2,1)} %all-to-all-done.2, s32[1024]{0:T(1024)S(1)} %pad_clamp_fusion), kind=kCustom, calls=%fused_computation.1 | custom fusion | bytes 25166080 | tf_op jit(solution)/shard_map/gather | solution.py:67
  186.4 9.3 %convolution_bitcast_fusion = bf16[64,128,768]{1,2,0:T(8,128)(2,1)} fusion(bf16[64,128,768]{2,1,0:T(8,128)(2,1)} %gather_fusion.1, bf16[1,1,64,128,128]{4,3,2,1,0:T(8,128)(2,1)S(1)} %copy-done), kind=kOutput, calls=%fused_computation.2 | convolution fusion | flops 1610612736 | bytes 27262976 | tf_op jit(solution)/shard_map/tji,tjf->tif/dot_general | solution.py:68
  195.6 16.8 %copy.48 = bf16[64,128,768]{2,0,1:T(8,128)(2,1)} copy(bf16[64,128,768]{1,2,0:T(8,128)(2,1)} %convolution_bitcast_fusion) | data formatting | bytes 25165824 | tf_op jit(solution)/shard_map/tji,tjf->tif/dot_general | solution.py:68
  212.5 6.3 %convolution_convert_fusion = bf16[8,128,768]{2,0,1:T(8,128)(2,1)S(1)} fusion(bf16[64,128,768]{2,0,1:T(8,128)(2,1)} %copy.48, s32[64]{0:T(128)S(1)} %bitcast.85, pred[64]{0:T(512)(128)(4,1)S(1)} %iota_compare_fusion.2), kind=kOutput, calls=%fused_computation.7 | convolution fusion | flops 100664320 | bytes 14156096 | tf_op jit(solution)/shard_map/kt,tif->kif/dot_general | solution.py:72
  218.8 1.5 copy.49
  220.3 38.3 %psum.15 = f32[1024]{0:T(1024)} all-reduce(f32[1024]{0:T(1024)S(1)} %get-tuple-element.4), channel_id=1, replica_groups=mesh['src'=4,'dst'=8] {'src','dst'}, use_global_device_ids=true, to_apply=%region_4.5 | all-reduce | flops 1024 | bytes 8192 | tf_op jit(solution)/shard_map/psum | solution.py:57
  258.7 31.1 %all-reduce.2.cloned.1.call-done = f32[768,1024]{1,0:T(8,128)} async-done(((f32[768,1024]{1,0:T(8,128)}), f32[768,1024]{1,0:T(8,128)}) %all-reduce.2.cloned.1.call-update) | async-done | bytes 3145744 | tf_op jit(solution)/shard_map/psum | solution.py:57
  289.7 29.9 %reduce-scatter.2.cloned.1.call-done = bf16[256,768]{1,0:T(8,128)(2,1)} async-done(((bf16[1024,768]{1,0:T(8,128)(2,1)}), bf16[256,768]{1,0:T(8,128)(2,1)}) %reduce-scatter.2.cloned.1.call-update) | async-done | bytes 393232 | tf_op jit(solution)/shard_map/reduce_scatter | solution.py:73
  319.6 4.0 %copy.63 = f32[768,1024]{1,0:T(8,128)} copy(f32[768,1024]{1,0:T(8,128)} %all-reduce.2.cloned.1.call-done) | data formatting | bytes 6291456
  (24 shorter events, 0.5 us)
Async XLA Ops:
  7.2 33.4 %copy-start = (bf16[1,1,64,128,128]{4,3,2,1,0:T(8,128)(2,1)S(1)}, bf16[1,1,64,128,128]{4,3,2,1,0:T(8,128)(2,1)}, u32[]{:S(2)}) copy-start(bf16[1,1,64,128,128]{4,3,2,1,0:T(8,128)(2,1)} %param.9) | copy-start | bytes 6291460
  7.2 24.8 %all-gather.2.cloned.1.call-start = ((), (), s32[]{:S(2)}) async-start(), calls=%async_computation.4 | async-start | bytes 1966080 | tf_op jit(solution)/shard_map/all_gather | solution.py:23
  10.0 64.2 %all-to-all-start.1 = ((s32[8,1,128]{2,1,0:T(1,128)}), s32[8,1,128]{2,1,0:T(1,128)S(1)}, u32[]{:S(2)}, u32[]{:S(2)}) async-start(s32[8,1,128]{2,1,0:T(1,128)} %broadcast_in_dim.16), calls=%async_computation.1 | async-start | bytes 8192 | tf_op jit(solution)/shard_map/all_to_all | solution.py:39
  74.3 43.0 %all-to-all-start = ((bf16[8,128,768]{2,1,0:T(8,128)(2,1)}), bf16[8,128,768]{2,1,0:T(8,128)(2,1)}, u32[]{:S(2)}, u32[]{:S(2)}) async-start(bf16[8,128,768]{2,1,0:T(8,128)(2,1)} %copy.41), calls=%async_computation | async-start | bytes 3145728 | tf_op jit(solution)/shard_map/all_to_all | solution.py:36
  79.8 40.5 %copy-start.3 = (bf16[256,1024]{1,0:T(8,128)(2,1)S(1)}, bf16[256,1024]{1,0:T(8,128)(2,1)}, u32[]{:S(2)}) copy-start(bf16[256,1024]{1,0:T(8,128)(2,1)} %param.15) | copy-start | bytes 1572868
  79.8 40.5 %copy-start.4 = (f32[1024]{0:T(1024)S(1)}, f32[1024]{0:T(1024)}, u32[]{:S(2)}) copy-start(f32[1024]{0:T(1024)} %param.14) | copy-start | bytes 12292
  120.3 3.3 %copy-start.2 = (bf16[768,1024]{1,0:T(8,128)(2,1)S(1)}, bf16[768,1024]{1,0:T(8,128)(2,1)}, u32[]{:S(2)}) copy-start(bf16[768,1024]{1,0:T(8,128)(2,1)} %param.13) | copy-start | bytes 4718596
  126.5 4.5 %copy-start.5 = (s32[1,1,64]{2,1,0:T(1,128)S(1)}, s32[1,1,64]{2,1,0:T(1,128)}, u32[]{:S(2)}) copy-start(s32[1,1,64]{2,1,0:T(1,128)} %param.11) | copy-start | bytes 772
  126.5 51.3 %all-to-all-start.2 = ((bf16[8,128,768]{2,1,0:T(8,128)(2,1)}), bf16[8,128,768]{2,1,0:T(8,128)(2,1)}, u32[]{:S(2)}, u32[]{:S(2)}) async-start(bf16[8,128,768]{2,1,0:T(8,128)(2,1)} %copy.46), calls=%async_computation.2 | async-start | bytes 3145728 | tf_op jit(solution)/shard_map/all_to_all | solution.py:66
  130.9 158.8 %all-reduce.2.cloned.1.call-start = ((), (), s32[]{:S(2)}) async-start(), calls=%async_computation.6 | async-start | bytes 6291456 | tf_op jit(solution)/shard_map/psum | solution.py:57
  133.3 186.4 %reduce-scatter.2.cloned.1.call-start = ((), (), s32[]{:S(2)}) async-start(), calls=%async_computation.5 | async-start | bytes 1966080 | tf_op jit(solution)/shard_map/reduce_scatter | solution.py:73
  195.6 16.8 %copy-start.1 = (s32[1,1,64]{2,1,0:T(1,128)S(1)}, s32[1,1,64]{2,1,0:T(1,128)}, u32[]{:S(2)}) copy-start(s32[1,1,64]{2,1,0:T(1,128)} %param.10) | copy-start | bytes 772
Sparse Core Ops, SparseCore 0:
  9.5 22.3 all-gather.1
  137.8 151.9 all-reduce.1
  292.8 26.7 reduce-scatter.1
where the time goes:
time: 331 us; the launch traced here: 330 us
  waiting for transfers between devices  157 us (47%)
  local copies, waits for them, and re-layouts  60.7 us (18%)
  matrix products  40.5 us (12%)
  blocking collectives  38.3 us (12%)
  starting transfers between devices  17.6 us (5%)
  between operations  14.5 us (4%)
    all_to_all x1, waiting for transfers between devices, per_device(): lax.all_to_all(replies, 'dst', split_axis=0, concat_axis=0, tiled=True)  44.2 us
    psum x1, blocking collectives, per_device(): weight_grad, bias_grad = lax.psum((weight_term, bias_term), ('src', 'dst'))  38.3 us
    all_to_all x1, waiting for transfers between devices, per_device(): lax.all_to_all(outgoing.astype(jnp.bfloat16), 'dst', split_axis=0, concat...  37.2 us
    psum x1, waiting for transfers between devices, per_device(): weight_grad, bias_grad = lax.psum((weight_term, bias_term), ('src', 'dst'))  31.1 us
    reduce_scatter x1, waiting for transfers between devices, per_device(): lax.psum_scatter(src_terms.reshape(holders * block_rows, feat_width).asty...  29.9 us
    dot_general x1, local copies, waits for them, and re-layouts, per_device(): jnp.einsum('tji,tjf->tif', adjacency, wanted, preferred_element_type=jnp....  16.8 us
    dot_general x1, local copies, waits for them, and re-layouts, per_device(): jnp.einsum('tij,tjf->tif', adjacency, picked, preferred_element_type=jnp....  16.8 us
    all_gather x1, waiting for transfers between devices, per_device(): lax.all_gather(features, 'src', axis=0, tiled=True)  14 us
  transfers between devices with their start and end apart: 6, of which 5 were waited for; matrix products, arithmetic and copies ran while one was open for 27% of the time, Pallas kernels for 0%

commit v1 on v0

--- a/solution.py
+++ b/solution.py
@@ -54,7 +54,7 @@
         "jrf,jrh->fh", aggregate, pre_grad_b, preferred_element_type=jnp.float32
     )
     bias_term = jnp.sum(pre_grad, axis=(0, 1))
-    weight_grad, bias_grad = lax.psum((weight_term, bias_term), ("src", "dst"))
+    weight_grad, bias_grad = lax.psum(lax.psum((weight_term, bias_term), "src"), "dst")
     back = jnp.einsum("jrh,fh->jrf", pre_grad_b, weight, preferred_element_type=jnp.float32).astype(
         jnp.bfloat16
     )

time: 331 us -> 378 us (1.14)
  waiting for transfers between devices: 157 us -> 214 us
  blocking collectives: 38.3 us -> 28.4 us
    psum x1 -> x2, waiting for transfers between devices: 31.1 us -> 132 us  [the longest x1 70.2 us: per_device(): lax.psum((weight_term, bias_term), 'src')]
    all_to_all x1, waiting for transfers between devices: 44.2 us -> 0.01 us  [per_device(): lax.all_to_all(replies, 'dst', split_axis=0, concat_axis=0, tiled=True)]
    psum x1 -> x2, blocking collectives: 38.3 us -> 28.4 us  [the longest x1 22.1 us: per_device(): lax.psum(lax.psum((weight_term, bias_term), 'src'), 'dst')]
  transfers between devices with their start and end apart: 6 -> 7, of which waited for: 5 -> 5; matrix products, arithmetic and copies ran while one was open for 27% -> 24% of each run, Pallas kernels for 0% -> 0%
where the time goes in v1:
time: 378 us; the launch traced here: 377 us
  waiting for transfers between devices  214 us (57%)
  local copies, waits for them, and re-layouts  60.6 us (16%)
  matrix products  40.6 us (11%)
  blocking collectives  28.4 us (8%)
  starting transfers between devices  17.6 us (5%)
  between operations  14.5 us (4%)
    psum x1, waiting for transfers between devices, per_device(): lax.psum((weight_term, bias_term), 'src')  70.2 us
    psum x1, waiting for transfers between devices, per_device(): lax.psum(lax.psum((weight_term, bias_term), 'src'), 'dst')  61.6 us
    all_to_all x1, waiting for transfers between devices, per_device(): lax.all_to_all(outgoing.astype(jnp.bfloat16), 'dst', split_axis=0, concat...  37.2 us
    reduce_scatter x1, waiting for transfers between devices, per_device(): lax.psum_scatter(src_terms.reshape(holders * block_rows, feat_width).asty...  30 us
    psum x1, blocking collectives, per_device(): lax.psum(lax.psum((weight_term, bias_term), 'src'), 'dst')  22.1 us
    dot_general x1, local copies, waits for them, and re-layouts, per_device(): jnp.einsum('tji,tjf->tif', adjacency, wanted, preferred_element_type=jnp....  16.8 us
    dot_general x1, local copies, waits for them, and re-layouts, per_device(): jnp.einsum('tij,tjf->tif', adjacency, picked, preferred_element_type=jnp....  16.7 us
    all_gather x1, waiting for transfers between devices, per_device(): lax.all_gather(features, 'src', axis=0, tiled=True)  14 us
  transfers between devices with their start and end apart: 7, of which 5 were waited for; matrix products, arithmetic and copies ran while one was open for 24% of the time, Pallas kernels for 0%

profile of v1, /device:TPU:0, one launch (start us, length us, event | category | flops | bytes accessed | tf_op | source)
XLA Modules:
  0.0 377.0 jit_solution(15636462644771644413)
XLA Ops:
  7.2 0.7 all-gather.2.cloned.1.call-update
  8.6 0.7 and_select_fusion.1
  9.4 0.7 broadcast_in_dim.16
  10.0 7.3 %all-to-all-start.1 = ((s32[8,1,128]{2,1,0:T(1,128)}), s32[8,1,128]{2,1,0:T(1,128)S(1)}, u32[]{:S(2)}, u32[]{:S(2)}) async-start(s32[8,1,128]{2,1,0:T(1,128)} %broadcast_in_dim.16), calls=%async_computation.1 | async-start | bytes 8192 | tf_op jit(solution)/shard_map/all_to_all | solution.py:39
  17.3 0.7 fusion.39
  18.0 14.0 %all-gather.2.cloned.1.call-done = bf16[1024,768]{1,0:T(8,128)(2,1)} async-done(((bf16[256,768]{1,0:T(8,128)(2,1)}), bf16[1024,768]{1,0:T(8,128)(2,1)}) %all-gather.2.cloned.1.call-update) | async-done | bytes 1572880 | tf_op jit(solution)/shard_map/all_gather | solution.py:23
  31.9 8.7 %gather_fusion = bf16[64,128,768]{2,1,0:T(8,128)(2,1)} fusion(bf16[8,128,768]{2,1,0:T(8,128)(2,1)} %bitcast.81, s32[1024]{0:T(1024)S(1)} %pad_clamp_fusion.1), kind=kCustom, calls=%fused_computation | custom fusion | bytes 25166080 | tf_op jit(solution)/shard_map/gather | solution.py:26
  40.6 9.1 %convolution_bitcast_fusion.1 = bf16[64,128,768]{1,2,0:T(8,128)(2,1)} fusion(bf16[64,128,768]{2,1,0:T(8,128)(2,1)} %gather_fusion, bf16[1,1,64,128,128]{4,3,2,1,0:T(8,128)(2,1)S(1)} %copy-done), kind=kOutput, calls=%fused_computation.3 | convolution fusion | flops 1610612736 | bytes 27262976 | tf_op jit(solution)/shard_map/tij,tjf->tif/dot_general | solution.py:27
  49.7 16.7 %copy.40 = bf16[64,128,768]{2,0,1:T(8,128)(2,1)} copy(bf16[64,128,768]{1,2,0:T(8,128)(2,1)} %convolution_bitcast_fusion.1) | data formatting | bytes 25165824 | tf_op jit(solution)/shard_map/tij,tjf->tif/dot_general | solution.py:27
  66.5 6.3 %convolution_convert_fusion.2 = bf16[8,128,768]{2,0,1:T(8,128)(2,1)S(1)} fusion(bf16[64,128,768]{2,0,1:T(8,128)(2,1)} %copy.40, s32[64]{0:T(128)S(1)} %get-tuple-element.8, pred[64]{0:T(512)(128)(4,1)S(1)} %iota_compare_fusion.2), kind=kOutput, calls=%fused_computation.9 | convolution fusion | flops 100664320 | bytes 14156096 | tf_op jit(solution)/shard_map/pt,tif->pif/dot_general | solution.py:33
  72.8 1.5 copy.41
  74.2 5.7 %all-to-all-start = ((bf16[8,128,768]{2,1,0:T(8,128)(2,1)}), bf16[8,128,768]{2,1,0:T(8,128)(2,1)}, u32[]{:S(2)}, u32[]{:S(2)}) async-start(bf16[8,128,768]{2,1,0:T(8,128)(2,1)} %copy.41), calls=%async_computation | async-start | bytes 3145728 | tf_op jit(solution)/shard_map/all_to_all | solution.py:36
  80.1 37.2 %all-to-all-done = bf16[8,128,768]{2,1,0:T(8,128)(2,1)} async-done(((bf16[8,128,768]{2,1,0:T(8,128)(2,1)}), bf16[8,128,768]{2,1,0:T(8,128)(2,1)}, u32[]{:S(2)}, u32[]{:S(2)}) %all-to-all-start) | async-done | bytes 1572896 | tf_op jit(solution)/shard_map/all_to_all | solution.py:36
  117.4 2.6 fusion.17
  119.9 0.5 copy.50
  120.4 3.3 fusion.42
  123.8 0.6 fusion.14
  124.4 0.7 convolution_convert_fusion.1
  125.1 1.4 copy.46
  126.6 4.3 %all-to-all-start.2 = ((bf16[8,128,768]{2,1,0:T(8,128)(2,1)}), bf16[8,128,768]{2,1,0:T(8,128)(2,1)}, u32[]{:S(2)}, u32[]{:S(2)}) async-start(bf16[8,128,768]{2,1,0:T(8,128)(2,1)} %copy.46), calls=%async_computation.2 | async-start | bytes 3145728 | tf_op jit(solution)/shard_map/all_to_all | solution.py:66
  130.9 2.2 convolution_bitcast_fusion.2
  133.2 70.2 %all-reduce.3.cloned.1.call-done = f32[768,1024]{1,0:T(8,128)} async-done(((f32[768,1024]{1,0:T(8,128)}), f32[768,1024]{1,0:T(8,128)}) %all-reduce.3.cloned.1.call-update) | async-done | bytes 3145744 | tf_op jit(solution)/shard_map/psum | solution.py:57
  203.8 8.6 %gather_fusion.1 = bf16[64,128,768]{2,1,0:T(8,128)(2,1)} fusion(bf16[8,128,768]{2,1,0:T(8,128)(2,1)} %all-to-all-done.2, s32[1024]{0:T(1024)S(1)} %pad_clamp_fusion), kind=kCustom, calls=%fused_computation.1 | custom fusion | bytes 25166080 | tf_op jit(solution)/shard_map/gather | solution.py:67
  212.4 9.4 %convolution_bitcast_fusion = bf16[64,128,768]{1,2,0:T(8,128)(2,1)} fusion(bf16[64,128,768]{2,1,0:T(8,128)(2,1)} %gather_fusion.1, bf16[1,1,64,128,128]{4,3,2,1,0:T(8,128)(2,1)S(1)} %copy-done), kind=kOutput, calls=%fused_computation.2 | convolution fusion | flops 1610612736 | bytes 27262976 | tf_op jit(solution)/shard_map/tji,tjf->tif/dot_general | solution.py:68
  221.8 16.8 %copy.48 = bf16[64,128,768]{2,0,1:T(8,128)(2,1)} copy(bf16[64,128,768]{1,2,0:T(8,128)(2,1)} %convolution_bitcast_fusion) | data formatting | bytes 25165824 | tf_op jit(solution)/shard_map/tji,tjf->tif/dot_general | solution.py:68
  238.6 6.4 %convolution_convert_fusion = bf16[8,128,768]{2,0,1:T(8,128)(2,1)S(1)} fusion(bf16[64,128,768]{2,0,1:T(8,128)(2,1)} %copy.48, s32[64]{0:T(128)S(1)} %bitcast.85, pred[64]{0:T(512)(128)(4,1)S(1)} %iota_compare_fusion.2), kind=kOutput, calls=%fused_computation.7 | convolution fusion | flops 100664320 | bytes 14156096 | tf_op jit(solution)/shard_map/kt,tif->kif/dot_general | solution.py:72
  245.0 1.5 copy.49
  246.5 6.3 %psum.30 = f32[1024]{0:T(1024)S(1)} all-reduce(f32[1024]{0:T(1024)S(1)} %get-tuple-element.4), channel_id=1, replica_groups=mesh['src'=4,'dst'=8] {'src'}, use_global_device_ids=true, to_apply=%region_5.6 | all-reduce | flops 1024 | bytes 8192 | tf_op jit(solution)/shard_map/psum | solution.py:57
  252.8 22.1 %psum.31 = f32[1024]{0:T(1024)} all-reduce(f32[1024]{0:T(1024)S(1)} %psum.30), channel_id=1, replica_groups=mesh['src'=4,'dst'=8] {'dst'}, use_global_device_ids=true, to_apply=%region_6.7 | all-reduce | flops 1024 | bytes 8192 | tf_op jit(solution)/shard_map/psum | solution.py:57
  274.9 61.6 %all-reduce.5.cloned.1.call-done = f32[768,1024]{1,0:T(8,128)} async-done(((f32[768,1024]{1,0:T(8,128)}), f32[768,1024]{1,0:T(8,128)}) %all-reduce.5.cloned.1.call-update) | async-done | bytes 3145744 | tf_op jit(solution)/shard_map/psum | solution.py:57
  336.4 30.0 %reduce-scatter.2.cloned.1.call-done = bf16[256,768]{1,0:T(8,128)(2,1)} async-done(((bf16[1024,768]{1,0:T(8,128)(2,1)}), bf16[256,768]{1,0:T(8,128)(2,1)}) %reduce-scatter.2.cloned.1.call-update) | async-done | bytes 393232 | tf_op jit(solution)/shard_map/reduce_scatter | solution.py:73
  366.5 4.0 %copy.64 = f32[768,1024]{1,0:T(8,128)} copy(f32[768,1024]{1,0:T(8,128)} %all-reduce.5.cloned.1.call-done) | data formatting | bytes 6291456
  (28 shorter events, 0.8 us)
Async XLA Ops:
  7.2 33.4 %copy-start = (bf16[1,1,64,128,128]{4,3,2,1,0:T(8,128)(2,1)S(1)}, bf16[1,1,64,128,128]{4,3,2,1,0:T(8,128)(2,1)}, u32[]{:S(2)}) copy-start(bf16[1,1,64,128,128]{4,3,2,1,0:T(8,128)(2,1)} %param.9) | copy-start | bytes 6291460
  7.2 24.8 %all-gather.2.cloned.1.call-start = ((), (), s32[]{:S(2)}) async-start(), calls=%async_computation.4 | async-start | bytes 1966080 | tf_op jit(solution)/shard_map/all_gather | solution.py:23
  10.0 64.2 %all-to-all-start.1 = ((s32[8,1,128]{2,1,0:T(1,128)}), s32[8,1,128]{2,1,0:T(1,128)S(1)}, u32[]{:S(2)}, u32[]{:S(2)}) async-start(s32[8,1,128]{2,1,0:T(1,128)} %broadcast_in_dim.16), calls=%async_computation.1 | async-start | bytes 8192 | tf_op jit(solution)/shard_map/all_to_all | solution.py:39
  74.2 46.2 %copy-start.3 = (bf16[256,1024]{1,0:T(8,128)(2,1)S(1)}, bf16[256,1024]{1,0:T(8,128)(2,1)}, u32[]{:S(2)}) copy-start(bf16[256,1024]{1,0:T(8,128)(2,1)} %param.15) | copy-start | bytes 1572868
  74.2 46.2 %copy-start.4 = (f32[1024]{0:T(1024)S(1)}, f32[1024]{0:T(1024)}, u32[]{:S(2)}) copy-start(f32[1024]{0:T(1024)} %param.14) | copy-start | bytes 12292
  74.2 43.1 %all-to-all-start = ((bf16[8,128,768]{2,1,0:T(8,128)(2,1)}), bf16[8,128,768]{2,1,0:T(8,128)(2,1)}, u32[]{:S(2)}, u32[]{:S(2)}) async-start(bf16[8,128,768]{2,1,0:T(8,128)(2,1)} %copy.41), calls=%async_computation | async-start | bytes 3145728 | tf_op jit(solution)/shard_map/all_to_all | solution.py:36
  120.4 3.3 copy-start.2
  126.6 77.2 %all-to-all-start.2 = ((bf16[8,128,768]{2,1,0:T(8,128)(2,1)}), bf16[8,128,768]{2,1,0:T(8,128)(2,1)}, u32[]{:S(2)}, u32[]{:S(2)}) async-start(bf16[8,128,768]{2,1,0:T(8,128)(2,1)} %copy.46), calls=%async_computation.2 | async-start | bytes 3145728 | tf_op jit(solution)/shard_map/all_to_all | solution.py:66
  130.9 72.6 %all-reduce.3.cloned.1.call-start = ((), (), s32[]{:S(2)}) async-start(), calls=%async_computation.6 | async-start | bytes 6291456 | tf_op jit(solution)/shard_map/psum | solution.py:57
  133.2 70.6 %copy-start.5 = (s32[1,1,64]{2,1,0:T(1,128)S(1)}, s32[1,1,64]{2,1,0:T(1,128)}, u32[]{:S(2)}) copy-start(s32[1,1,64]{2,1,0:T(1,128)} %param.11) | copy-start | bytes 772
  133.2 203.3 %all-reduce.5.cloned.1.call-start = ((), (), s32[]{:S(2)}) async-start(), calls=%async_computation.7 | async-start | bytes 6291456 | tf_op jit(solution)/shard_map/psum | solution.py:57
  203.5 163.0 %reduce-scatter.2.cloned.1.call-start = ((), (), s32[]{:S(2)}) async-start(), calls=%async_computation.5 | async-start | bytes 1966080 | tf_op jit(solution)/shard_map/reduce_scatter | solution.py:73
  221.8 16.8 %copy-start.1 = (s32[1,1,64]{2,1,0:T(1,128)S(1)}, s32[1,1,64]{2,1,0:T(1,128)}, u32[]{:S(2)}) copy-start(s32[1,1,64]{2,1,0:T(1,128)} %param.10) | copy-start | bytes 772
Sparse Core Ops, SparseCore 0:
  9.5 22.3 all-gather.1
  134.6 68.8 all-reduce.2
  207.1 129.3 all-reduce.4
  339.4 27.0 reduce-scatter.1
